TPU v7x, 32 devices: a whole 2x2x4 slice. The times are simulated.
32 devices in a mesh: trow: 4 (over y, core), tcol: 8 (over z, x).
Axes of the slice: x: 2, y: 2, z: 4, core: 2. Of those that a mesh axis runs over, the one named last changes fastest.
Arguments:
- response: bfloat16 [4096, 16384], P('trow', 'tcol'), may hold values from -0.046875 to 0.046875
- test_matrix: bfloat16 [1024, 192], P(('trow', 'tcol')), may hold values from -6 to 6
- slopes: bfloat16 [16384, 256], P('tcol', 'trow'), may hold values from -6 to 6
- ranks: int32 [4, 16], P('trow', 'tcol'), may hold values from 16 to 192, as said below
Outputs:
- commands: float32 [4096, 256], P(('trow', 'tcol'))
Inputs may be any that keep to these rules, and one draw needn't show every extreme that they name: ranks of tiles near the diagonal tend to be higher, and every tile's sketch has full column rank and is well conditioned.
All inputs are finite; a program needn't handle non-finite values.
Results may differ from a plain program's by a relative error of at most 0.014.
Values may be sent and summed in bfloat16 or wider, within the bound.
A program may use at most 64 MiB of HBM per device.

v0:
```python
import jax
import jax.numpy as jnp
from jax import lax
from jax.sharding import PartitionSpec as P


def fetch_frames(slopes):
    return lax.all_gather(slopes, "trow", axis=1, tiled=True)


def on_device(response, test_matrix, slopes, ranks):
    highest = lax.Precision.HIGHEST
    tile_rows = ranks.shape[0]
    tile_cols = ranks.shape[1]
    width = response.shape[0] // tile_rows
    sketch_width = test_matrix.shape[1]
    tiles = response.reshape(tile_rows, width, tile_cols, width)
    row_block = lax.all_gather(test_matrix, "tcol", axis=0, tiled=True)
    sketch = jnp.einsum(
        "rick,kj->rcij",
        tiles,
        lax.all_gather(row_block, "trow", axis=0, tiled=True),
        preferred_element_type=jnp.float32,
    )
    gram = jnp.einsum("rcik,rcil->rckl", sketch, sketch, precision=highest)
    chol = jnp.linalg.cholesky(gram)
    basis = jax.scipy.linalg.solve_triangular(chol, jnp.swapaxes(sketch, 2, 3), lower=True)
    slots = jnp.arange(sketch_width, dtype=jnp.int32)
    keep = (slots[None, None, :] < ranks[:, :, None]).astype(jnp.float32)
    basis = (basis * keep[:, :, :, None]).astype(jnp.bfloat16)
    factor = jnp.einsum("rcsi,ricj->rcsj", basis, tiles, preferred_element_type=jnp.float32).astype(
        jnp.bfloat16
    )
    frames = fetch_frames(slopes)
    frame_count = frames.shape[1]
    frame_tiles = frames.reshape(tile_cols, width, frame_count)
    coeff = jnp.einsum(
        "rcsj,cjf->rcsf", factor, frame_tiles, preferred_element_type=jnp.float32
    ).astype(jnp.bfloat16)
    share_rows = tile_rows * width // lax.axis_size("tcol")
    summed = jnp.einsum("rcsi,rcsf->rif", basis, coeff, preferred_element_type=jnp.float32)
    summed_all = lax.psum(
        summed.reshape(tile_rows * width, frame_count).astype(jnp.bfloat16), "tcol"
    ).astype(jnp.float32)
    result = lax.dynamic_slice_in_dim(
        summed_all, lax.axis_index("tcol") * share_rows, share_rows, 0
    )
    return result


def solution(mesh):
    return jax.shard_map(
        on_device,
        mesh=mesh,
        in_specs=(
            P("trow", "tcol"),
            P(("trow", "tcol"), None),
            P("tcol", "trow"),
            P("trow", "tcol"),
        ),
        out_specs=P(("trow", "tcol"), None),
        check_vma=False,
    )
```

profile of v0, /device:TPU:0, one launch (start us, length us, event | category | flops | bytes accessed | tf_op | source)
XLA Modules:
  0.0 238.7 jit_solution(7302587469162838817)
XLA Ops:
  6.5 0.0 all-gather.2.cloned.1.call-start
  6.5 0.7 all-gather.2.cloned.1.call-update
  7.3 0.0 all-reduce.5.cloned.1.call-start
  7.4 32.5 %all_gather.9 = bf16[256,192]{1,0:T(8,128)(2,1)S(1)} all-gather(bf16[32,192]{1,0:T(8,128)(2,1)} %param.5), channel_id=1, replica_groups=mesh['trow'=4,'tcol'=8] {'tcol'}, dimensions={0}, use_global_device_ids=true | all-gather | bytes 110592 | tf_op jit(solution)/shard_map/all_gather | solution.py:18
  39.9 0.1 copy.21
  40.1 6.5 %all_gather.10 = bf16[1024,192]{0,1:T(8,128)(2,1)S(1)} all-gather(bf16[256,192]{0,1:T(8,128)(2,1)S(1)} %copy.21), channel_id=1, replica_groups=mesh['trow'=4,'tcol'=8] {'trow'}, dimensions={0}, use_global_device_ids=true | all-gather | bytes 491520 | tf_op jit(solution)/shard_map/all_gather | solution.py:22
  46.5 3.7 %fusion.2 = f32[192,1024,2]{1,0,2:T(8,128)S(1)} fusion(bf16[128,2,8,1024]{3,2,1,0:T(8,128)(2,1)} %bitcast.77, bf16[1024,192]{0,1:T(8,128)(2,1)S(1)} %all_gather.10), kind=kOutput, calls=%fused_computation.2 | convolution fusion | flops 805306368 | bytes 6160384 | tf_op jit(solution)/shard_map/rick,kj->rcij/dot_general | solution.py:19
  50.3 1.7 fusion.7
  51.9 0.2 copy.24
  52.1 0.1 fusion.16
  52.2 23.6 %custom-call.17 = f32[1,2,128,128]{3,2,1,0:T(8,128)S(1)} custom-call(f32[1,2,128,128]{3,2,1,0:T(8,128)S(1)} %cholesky.132), custom_call_target="Cholesky" | custom-call | tf_op jit(solution)/shard_map/jit(cholesky)/cholesky | solution.py:26
  75.9 19.7 %custom-call.18 = f32[1,2,1,128,128]{3,4,2,1,0:T(8,128)S(1)} custom-call(f32[1,2,1,128,128]{4,3,2,1,0:T(8,128)S(1)} %get-tuple-element.26), custom_call_target="InvertDiagBlocksLowerTriangular" | custom-call | tf_op jit(solution)/shard_map/jit(cholesky)/cholesky | solution.py:26
  95.6 0.0 copy-start
  95.6 0.2 bitcast_dynamic-update-slice_fusion
  95.9 0.2 fusion.13
  96.1 11.7 %custom-call.19 = f32[1,2,64,64]{3,2,1,0:T(8,128)S(1)} custom-call(f32[1,2,64,64]{3,2,1,0:T(8,128)S(1)} %fusion.13), custom_call_target="Cholesky" | custom-call | tf_op jit(solution)/shard_map/jit(cholesky)/cholesky | solution.py:26
  107.9 0.1 compare_reduce_fusion
  108.0 0.1 compare_reduce_fusion.1
  108.1 0.1 bitcast_select_fusion
  108.3 0.1 fusion.18
  108.5 39.5 %custom-call.20 = f32[2,2,128,128]{2,3,1,0:T(8,128)S(1)} custom-call(f32[2,2,128,128]{3,2,1,0:T(8,128)S(1)} %pad_maximum_fusion), custom_call_target="InvertDiagBlocksLowerTriangular" | custom-call | tf_op jit(solution)/shard_map/jit(_solve_triangular)/vmap()/triangular_solve | solution.py:27
  148.0 0.0 copy-done
  148.0 0.1 compare_convert_fusion
  148.1 0.0 copy-start.1
  148.1 1.1 fusion.14
  149.2 0.7 convolution_subtract_fusion
  149.9 0.6 fusion.22
  150.5 0.0 copy-done.1
  150.5 2.0 fusion.9
  152.5 0.0 all-gather.2.cloned.1.call-done
  152.5 1.5 copy.30
  154.0 2.8 %fusion.12 = bf16[1024,256]{1,0:T(8,128)(2,1)} fusion(bf16[2,192,1024]{2,1,0:T(8,128)(2,1)} %fusion.9, bf16[2,1024,256]{2,1,0:T(8,128)(2,1)S(1)} %bitcast.75, f32[2,64,1024]{2,1,0:T(8,128)S(1)} %fusion.22, f32[2,128,1024]{2,1,0:T(8,128)S(1)} %fusion.14, f32[2,192]{1,0:T(2,128)S(1)} %compare_convert_fusion), kind=kOutput, calls=%fused_computation.12 | convolution fusion | flops 404193280 | bytes 3933696 | tf_op jit(solution)/shard_map/rcsi,rcsf->rif/dot_general | solution.py:41
  156.8 0.0 all-reduce.5.cloned.1.call-update
  156.8 73.5 %all-reduce.5.cloned.1.call-done = bf16[1024,256]{1,0:T(8,128)(2,1)} async-done(((bf16[1024,256]{1,0:T(8,128)(2,1)}), bf16[1024,256]{1,0:T(8,128)(2,1)}) %all-reduce.5.cloned.1.call-update) | async-done | bytes 524304 | tf_op jit(solution)/shard_map/psum | solution.py:42
  230.3 1.5 dynamic-slice_convert_fusion
  (14 shorter events, 0.2 us)
Async XLA Ops:
  6.5 146.0 %all-gather.2.cloned.1.call-start = ((), (), s32[]{:S(2)}) async-start(), calls=%async_computation | async-start | bytes 1310720 | tf_op jit(solution)/shard_map/all_gather | solution.py:8
  7.3 223.1 %all-reduce.5.cloned.1.call-start = ((), (), s32[]{:S(2)}) async-start(), calls=%async_computation.1 | async-start | bytes 1048576 | tf_op jit(solution)/shard_map/psum | solution.py:42
  95.6 52.4 %copy-start = (s32[1,2]{1,0:T(1,128)S(1)}, s32[1,2]{1,0:T(1,128)}, u32[]{:S(2)}) copy-start(s32[1,2]{1,0:T(1,128)} %param.7) | copy-start | bytes 28
  148.1 2.4 %copy-start.1 = (bf16[1024,2048]{1,0:T(8,128)(2,1)S(1)}, bf16[1024,2048]{1,0:T(8,128)(2,1)}, u32[]{:S(2)}) copy-start(bf16[1024,2048]{1,0:T(8,128)(2,1)} %param.4) | copy-start | bytes 12582916
Sparse Core Ops, SparseCore 0:
  8.9 19.4 all-gather.1
  156.9 73.3 all-reduce.4
where the time goes:
time: 239 us
  other arithmetic  96.8 us (41%)
  waiting for transfers between devices  74.2 us (31%)
  blocking collectives  39 us (16%)
  between operations  13.6 us (6%)
  matrix products  13 us (5%)
    psum x1, waiting for transfers between devices, on_device(): lax.psum(summed.reshape(tile_rows * width, frame_count).astype(jnp.bfloat...  73.5 us
    another operation x10, other arithmetic, on_device(): chol = jnp.linalg.cholesky(gram)  55.4 us
    another operation x7, other arithmetic, on_device(): jax.scipy.linalg.solve_triangular(chol, jnp.swapaxes(sketch, 2, 3), lower...  39.8 us
    all_gather x1, blocking collectives, on_device(): row_block = lax.all_gather(test_matrix, 'tcol', axis=0, tiled=True)  32.5 us
    all_gather x1, blocking collectives, on_device(): lax.all_gather(row_block, 'trow', axis=0, tiled=True)  6.49 us
  transfers between devices with their start and end apart: 2, of which 1 were waited for; matrix products, arithmetic and copies ran while one was open for 44% of the time, Pallas kernels for 0%

commit v1 on v0

--- a/solution.py
+++ b/solution.py
@@ -16,12 +16,38 @@
     sketch_width = test_matrix.shape[1]
     tiles = response.reshape(tile_rows, width, tile_cols, width)
     row_block = lax.all_gather(test_matrix, "tcol", axis=0, tiled=True)
-    sketch = jnp.einsum(
+    size, position, rows = (lax.axis_size("trow"), lax.axis_index("trow"), row_block.shape[0])
+    right = [(i, (i + 1) % size) for i in range(size)]
+    left = [(i, (i - 1) % size) for i in range(size)]
+    halfway = size // 2
+    from_left = from_right = row_block
+    subtotal = jnp.einsum(
         "rick,kj->rcij",
-        tiles,
-        lax.all_gather(row_block, "trow", axis=0, tiled=True),
+        lax.dynamic_slice_in_dim(tiles, position * rows, row_block.shape[0], axis=3),
+        row_block,
         preferred_element_type=jnp.float32,
     )
+    for step in range(1, halfway + 1):
+        from_left = lax.ppermute(from_left, "trow", right)
+        if step < size - halfway:
+            from_right = lax.ppermute(from_right, "trow", left)
+            subtotal = subtotal + jnp.einsum(
+                "rick,kj->rcij",
+                lax.dynamic_slice_in_dim(
+                    tiles, (position + step) % size * rows, from_right.shape[0], axis=3
+                ),
+                from_right,
+                preferred_element_type=jnp.float32,
+            )
+        subtotal = subtotal + jnp.einsum(
+            "rick,kj->rcij",
+            lax.dynamic_slice_in_dim(
+                tiles, (position - step) % size * rows, from_left.shape[0], axis=3
+            ),
+            from_left,
+            preferred_element_type=jnp.float32,
+        )
+    sketch = subtotal
     gram = jnp.einsum("rcik,rcil->rckl", sketch, sketch, precision=highest)
     chol = jnp.linalg.cholesky(gram)
     basis = jax.scipy.linalg.solve_triangular(chol, jnp.swapaxes(sketch, 2, 3), lower=True)

time: 239 us -> 249 us (1.042)
  local copies, waits for them, and re-layouts: 1.83 us -> 14.2 us
  blocking collectives: 39 us -> 32.5 us
  waiting for transfers between devices: 74.2 us -> 77.2 us
    reshape x0 -> x2, local copies, waits for them, and re-layouts: none -> 9.27 us  [the longest x1 7.8 us: on_device(): tiles = response.reshape(tile_rows, width, tile_cols, width)]
    all_gather x1 -> x0, blocking collectives: 6.49 us -> none  [on_device(): lax.all_gather(row_block, 'trow', axis=0, tiled=True)]
    dynamic_slice x0 -> x1, local copies, waits for them, and re-layouts: none -> 4.58 us  [on_device(): lax.dynamic_slice_in_dim(tiles, (position - step) % size * rows, from_lef...]
    ppermute x0 -> x3, waiting for transfers between devices: none -> 3.36 us  [the longest x2 3.36 us: on_device(): from_left = lax.ppermute(from_left, 'trow', right)]
  transfers between devices with their start and end apart: 2 -> 5, of which waited for: 1 -> 2; matrix products, arithmetic and copies ran while one was open for 44% -> 47% of each run, Pallas kernels for 0% -> 0%
where the time goes in v1:
time: 249 us; the launch traced here: 248 us
  other arithmetic  96.8 us (39%)
  waiting for transfers between devices  77.2 us (31%)
  blocking collectives  32.5 us (13%)
  local copies, waits for them, and re-layouts  14.2 us (6%)
  between operations  13.7 us (6%)
  matrix products  12.1 us (5%)
    psum x1, waiting for transfers between devices, on_device(): lax.psum(summed.reshape(tile_rows * width, frame_count).astype(jnp.bfloat...  73.8 us
    another operation x10, other arithmetic, on_device(): chol = jnp.linalg.cholesky(gram)  55.4 us
    another operation x7, other arithmetic, on_device(): jax.scipy.linalg.solve_triangular(chol, jnp.swapaxes(sketch, 2, 3), lower...  39.8 us
    all_gather x1, blocking collectives, on_device(): row_block = lax.all_gather(test_matrix, 'tcol', axis=0, tiled=True)  32.5 us
    reshape x1, local copies, waits for them, and re-layouts, on_device(): tiles = response.reshape(tile_rows, width, tile_cols, width)  7.8 us
  transfers between devices with their start and end apart: 5, of which 2 were waited for; matrix products, arithmetic and copies ran while one was open for 47% of the time, Pallas kernels for 0%

profile of v1, /device:TPU:0, one launch (start us, length us, event | category | flops | bytes accessed | tf_op | source)
XLA Modules:
  0.0 248.5 jit_solution(6105250592057757985)
XLA Ops:
  6.5 0.0 all-gather.2.cloned.1.call-start
  6.5 32.5 %all_gather.6 = bf16[256,192]{1,0:T(8,128)(2,1)S(1)} all-gather(bf16[32,192]{1,0:T(8,128)(2,1)} %param.5), channel_id=1, replica_groups=mesh['trow'=4,'tcol'=8] {'tcol'}, dimensions={0}, use_global_device_ids=true | all-gather | bytes 110592 | tf_op jit(solution)/shard_map/all_gather | solution.py:18
  39.1 0.0 collective-permute-start.1
  39.1 1.7 collective-permute-start
  40.8 0.0 all-gather.2.cloned.1.call-update
  40.8 0.0 all-reduce.5.cloned.1.call-start
  41.0 7.8 %reshape.154 = bf16[1,1024,2,1024]{3,2,1,0:T(2,128)(2,1)} reshape(bf16[1024,2048]{1,0:T(8,128)(2,1)} %param.4) | data formatting | bytes 8388608 | tf_op jit(solution)/shard_map/reshape | solution.py:17
  48.8 4.6 %constant_dynamic-slice_fusion = (bf16[1,1024,2,256]{3,2,1,0:T(2,128)(2,1)S(1)}, bf16[1,1024,2,256]{3,2,1,0:T(2,128)(2,1)S(1)}, bf16[1,1024,2,256]{3,2,1,0:T(2,128)(2,1)S(1)}, bf16[1,1024,2,256]{3,2,1,0:T(2,128)(2,1)S(1)}) fusion(bf16[1,1024,2,1024]{3,2,1,0:T(2,128)(2,1)} %reshape.154, s32[]{:T(128)S(6)} %select_n.40, s32[]{:T(128)S(6)} %select_n.38, ...), kind=kLoop, calls=%fused_computation.59 | loop fusion | bytes 8388624 | tf_op jit(solution)/shard_map/dynamic_slice | solution.py:44
  53.4 0.0 copy-start.2
  53.4 0.5 fusion.15
  53.9 0.1 copy-done.2
  54.1 0.1 compare_convert_fusion
  54.2 0.0 collective-permute-done.1
  54.2 0.1 collective-permute-start.2
  54.2 0.5 fusion.13
  54.7 0.0 collective-permute-done
  54.7 0.5 fusion.14
  55.3 3.4 %collective-permute-done.2 = bf16[256,192]{1,0:T(8,128)(2,1)S(1)} collective-permute-done((bf16[256,192]{1,0:T(8,128)(2,1)S(1)}, bf16[256,192]{1,0:T(8,128)(2,1)S(1)}, u32[]{:S(2)}, u32[]{:S(2)}) %collective-permute-start.2) | collective-permute-done | bytes 98336 | tf_op jit(solution)/shard_map/ppermute | solution.py:31
  58.6 0.5 add_add_fusion
  59.1 1.7 fusion.4
  60.8 0.2 copy.26
  61.0 0.1 fusion.17
  61.1 23.6 %custom-call.17 = f32[1,2,128,128]{3,2,1,0:T(8,128)S(1)} custom-call(f32[1,2,128,128]{3,2,1,0:T(8,128)S(1)} %cholesky.132), custom_call_target="Cholesky" | custom-call | tf_op jit(solution)/shard_map/jit(cholesky)/cholesky | solution.py:52
  84.8 19.7 %custom-call.18 = f32[1,2,1,128,128]{3,4,2,1,0:T(8,128)S(1)} custom-call(f32[1,2,1,128,128]{4,3,2,1,0:T(8,128)S(1)} %get-tuple-element.30), custom_call_target="InvertDiagBlocksLowerTriangular" | custom-call | tf_op jit(solution)/shard_map/jit(cholesky)/cholesky | solution.py:52
  104.5 0.2 bitcast_dynamic-update-slice_fusion
  104.7 0.2 fusion.10
  105.0 11.7 %custom-call.19 = f32[1,2,64,64]{3,2,1,0:T(8,128)S(1)} custom-call(f32[1,2,64,64]{3,2,1,0:T(8,128)S(1)} %fusion.10), custom_call_target="Cholesky" | custom-call | tf_op jit(solution)/shard_map/jit(cholesky)/cholesky | solution.py:52
  116.7 0.1 compare_reduce_fusion
  116.8 0.1 compare_reduce_fusion.1
  117.0 0.1 bitcast_select_fusion
  117.1 0.1 fusion.18
  117.3 39.5 %custom-call.20 = f32[2,2,128,128]{2,3,1,0:T(8,128)S(1)} custom-call(f32[2,2,128,128]{3,2,1,0:T(8,128)S(1)} %pad_maximum_fusion), custom_call_target="InvertDiagBlocksLowerTriangular" | custom-call | tf_op jit(solution)/shard_map/jit(_solve_triangular)/vmap()/triangular_solve | solution.py:53
  156.8 0.0 copy-start.1
  156.8 0.0 copy-start
  156.9 1.1 fusion.11
  157.9 0.0 copy-done.1
  157.9 0.7 fusion.25
  158.6 1.5 fusion.16
  160.1 0.0 copy-done
  160.2 1.9 fusion.6
  162.1 0.0 all-gather.2.cloned.1.call-done
  162.1 1.5 copy.43
  163.6 2.8 %fusion.9 = bf16[1024,256]{1,0:T(8,128)(2,1)} fusion(bf16[2,192,1024]{2,1,0:T(8,128)(2,1)} %fusion.6, bf16[2,1024,256]{2,1,0:T(8,128)(2,1)S(1)} %bitcast.96, f32[2,64,1024]{2,1,0:T(8,128)S(1)} %fusion.16, f32[2,128,1024]{2,1,0:T(8,128)S(1)} %fusion.11, f32[2,192]{1,0:T(2,128)S(1)} %compare_convert_fusion), kind=kOutput, calls=%fused_computation.10 | convolution fusion | flops 404193280 | bytes 3933696 | tf_op jit(solution)/shard_map/rcsi,rcsf->rif/dot_general | solution.py:67
  166.3 0.0 all-reduce.5.cloned.1.call-update
  166.3 73.8 %all-reduce.5.cloned.1.call-done = bf16[1024,256]{1,0:T(8,128)(2,1)} async-done(((bf16[1024,256]{1,0:T(8,128)(2,1)}), bf16[1024,256]{1,0:T(8,128)(2,1)}) %all-reduce.5.cloned.1.call-update) | async-done | bytes 524304 | tf_op jit(solution)/shard_map/psum | solution.py:68
  240.1 1.5 dynamic-slice_convert_fusion
  (14 shorter events, 0.2 us)
Async XLA Ops:
  6.5 155.6 %all-gather.2.cloned.1.call-start = ((), (), s32[]{:S(2)}) async-start(), calls=%async_computation | async-start | bytes 1310720 | tf_op jit(solution)/shard_map/all_gather | solution.py:8
  39.1 15.1 %collective-permute-start.1 = (bf16[256,192]{1,0:T(8,128)(2,1)S(1)}, bf16[256,192]{1,0:T(8,128)(2,1)S(1)}, u32[]{:S(2)}, u32[]{:S(2)}) collective-permute-start(bf16[256,192]{1,0:T(8,128)(2,1)S(1)} %all_gather.6), channel_id=1, source_target_pairs={{0,8},{8,16},{16,24},{24,0},{1,9},{9,17},{17,25},{25,1},{2,10},{10... | collective-permute-start | bytes 294920 | tf_op jit(solution)/shard_map/ppermute | solution.py:31
  39.1 15.7 %collective-permute-start = (bf16[256,192]{1,0:T(8,128)(2,1)S(1)}, bf16[256,192]{1,0:T(8,128)(2,1)S(1)}, u32[]{:S(2)}, u32[]{:S(2)}) collective-permute-start(bf16[256,192]{1,0:T(8,128)(2,1)S(1)} %all_gather.6), channel_id=1, source_target_pairs={{0,24},{8,0},{16,8},{24,16},{1,25},{9,1},{17,9},{25,17},{2,26},{10... | collective-permute-start | bytes 294920 | tf_op jit(solution)/shard_map/ppermute | solution.py:33
  40.8 199.3 %all-reduce.5.cloned.1.call-start = ((), (), s32[]{:S(2)}) async-start(), calls=%async_computation.1 | async-start | bytes 1048576 | tf_op jit(solution)/shard_map/psum | solution.py:68
  53.4 0.7 copy-start.2
  54.2 4.4 %collective-permute-start.2 = (bf16[256,192]{1,0:T(8,128)(2,1)S(1)}, bf16[256,192]{1,0:T(8,128)(2,1)S(1)}, u32[]{:S(2)}, u32[]{:S(2)}) collective-permute-start(bf16[256,192]{1,0:T(8,128)(2,1)S(1)} %collective-permute-done.1), channel_id=1, source_target_pairs={{0,8},{8,16},{16,24},{24,0},{1,9},{9,17},{17,25},{25,1},{2,10},{10... | collective-permute-start | bytes 294920 | tf_op jit(solution)/shard_map/ppermute | solution.py:31
  156.8 1.1 copy-start.1
  156.8 3.3 %copy-start = (bf16[1024,2048]{1,0:T(8,128)(2,1)S(1)}, bf16[1024,2048]{1,0:T(8,128)(2,1)}, u32[]{:S(2)}) copy-start(bf16[1024,2048]{1,0:T(8,128)(2,1)} %param.4) | copy-start | bytes 12582916
Sparse Core Ops, SparseCore 0:
  41.0 17.5 all-gather.1
  166.5 73.5 all-reduce.4
